TPU v7x, 32 devices: a whole 2x2x4 slice. The times are simulated.
32 devices in a mesh: occ: 4 (over y, core), aux: 8 (over z, x).
Axes of the slice: x: 2, y: 2, z: 4, core: 2. Of those that a mesh axis runs over, the one named last changes fastest.
Arguments:
- pair_ints: bfloat16 [16, 128, 20480], P(None, None, ('aux', 'occ')), may hold values from -110 to 110
- domain_len: int32 [4], replicated, may hold values from 1 to 4, as said below
- domain_blocks: int32 [4, 4], replicated, may hold values from 0 to 703
- slot_orbital: int32 [4], replicated, may hold values from 0 to 3, each once
- virt_energy: float32 [90112], replicated, may hold values from 0.1 to 3
- occ_energy: float32 [4], replicated, may hold values from -2 to -0.3
Outputs:
- projected: bfloat16 [4, 512, 20480], P('occ', None, 'aux')
Inputs may be any that keep to these rules, and one draw needn't show every extreme that they name: `domain_len`: some orbital has exactly 4 live blocks. `slot_orbital`: each orbital is owned by exactly one group.
All inputs are finite; a program needn't handle non-finite values.
Results may differ from a plain program's by a relative error of at most 0.001.
The roundings to bfloat16 on the way count: a program that leaves them out, or rounds other values in their place, can miss the bound.
Values may be sent and summed in bfloat16 or wider, within the bound.
A program may use at most 128 MiB of HBM per device.

v0:
```python
import jax
import jax.numpy as jnp
from jax import lax
from jax.sharding import PartitionSpec as P

LEVEL_RATIO = 0.5
EPSILON = 1e-05


def local(pair_ints, domain_len, domain_blocks, slot_orbital, virt_energy, occ_energy):
    orbitals = domain_len.shape[0]
    block_count = domain_blocks.shape[1]
    block_rows = pair_ints.shape[1]
    local_cols = pair_ints.shape[2]
    domain_size = block_count * block_rows
    slot_ids = jnp.arange(block_count, dtype=jnp.int32)
    ordered_len = jnp.take(domain_len, slot_orbital, axis=0)
    starts = (slot_orbital * block_count)[:, None] + slot_ids[None, :]
    live_mask = slot_ids[None, :] < ordered_len[:, None]
    flat_index = starts.reshape(-1)
    picked = jnp.take(pair_ints, flat_index, axis=0)
    picked = jnp.where(live_mask.reshape(-1)[:, None, None], picked, jnp.zeros_like(picked))
    padded = picked.reshape(orbitals, domain_size, local_cols)
    regrouped = lax.all_to_all(padded, "occ", split_axis=0, concat_axis=2, tiled=True)
    own_rows = regrouped[0]
    owner_group = lax.axis_index("occ")
    orbital = lax.dynamic_index_in_dim(slot_orbital, owner_group, 0, keepdims=False)
    partials = jnp.einsum("oac,obc->oab", padded, padded, preferred_element_type=jnp.float32)
    gram_part = lax.psum_scatter(
        partials.reshape(orbitals * domain_size, domain_size),
        ("occ", "aux"),
        scatter_dimension=0,
        tiled=True,
    )
    gram_sum = lax.all_gather(gram_part, "aux", axis=0, tiled=True)
    energy_table = virt_energy.reshape(-1, block_rows)
    blocks = lax.dynamic_index_in_dim(domain_blocks, orbital, 0, keepdims=False)
    energies = jnp.take(energy_table, blocks, axis=0).reshape(domain_size)
    occ_level = lax.dynamic_index_in_dim(occ_energy, orbital, 0, keepdims=False)
    denominator = energies[:, None] + energies[None, :] - 2.0 * occ_level
    amplitude = gram_sum / denominator
    length = lax.dynamic_index_in_dim(domain_len, orbital, 0, keepdims=False).astype(jnp.float32)
    level_shift = LEVEL_RATIO * (jnp.trace(amplitude) / (block_rows * length) + EPSILON)
    factor = jnp.linalg.cholesky(amplitude + level_shift * jnp.eye(domain_size, dtype=jnp.float32))
    solved = jax.scipy.linalg.cho_solve((factor, True), amplitude)
    projector = solved.T.astype(jnp.bfloat16)
    projected = jnp.dot(projector, own_rows, preferred_element_type=jnp.float32).astype(
        jnp.bfloat16
    )
    return projected[None]


def solution(mesh):
    placed = (P(None, None, ("aux", "occ")), P(), P(), P(), P(), P())
    return jax.shard_map(
        local, mesh=mesh, in_specs=placed, out_specs=P("occ", None, "aux"), check_vma=False
    )
```

profile of v0, /device:TPU:0, one launch (start us, length us, event | category | flops | bytes accessed | tf_op | source)
XLA Modules:
  0.0 390.7 jit_solution(3105162862275415704)
XLA Ops:
  9.7 2.4 gather_fusion.1
  14.2 3.8 fusion.62
  18.1 4.7 %all-to-all-start = ((bf16[4,512,640]{2,1,0:T(8,128)(2,1)}), bf16[4,512,640]{2,1,0:T(8,128)(2,1)}, u32[]{:S(2)}, u32[]{:S(2)}) async-start(bf16[4,512,640]{2,1,0:T(8,128)(2,1)} %copy-done.2), calls=%async_computation | async-start | bytes 5242880 | tf_op jit(solution)/shard_map/all_to_all | solution.py:24
  22.8 143.1 %reduce-scatter.4.cloned.1.call-done = f32[64,512]{1,0:T(8,128)} async-done(((f32[2048,512]{1,0:T(8,128)}), f32[64,512]{1,0:T(8,128)}) %reduce-scatter.4.cloned.1.call-update) | async-done | bytes 131088 | tf_op jit(solution)/shard_map/reduce_scatter | solution.py:29
  173.1 4.8 %copy.58 = bf16[1,512,4,640]{1,3,2,0:T(8,128)(2,1)} copy(bf16[1,512,4,640]{3,1,2,0:T(8,128)(2,1)} %bitcast.23) | data formatting | bytes 5242880 | tf_op jit(solution)/shard_map/all_to_all | solution.py:24
  177.9 28.2 %all-gather.2.cloned.1.call-done = f32[512,512]{1,0:T(8,128)} async-done(((f32[64,512]{1,0:T(8,128)}), f32[512,512]{1,0:T(8,128)}) %all-gather.2.cloned.1.call-update) | async-done | bytes 1048592 | tf_op jit(solution)/shard_map/all_gather | solution.py:35
  206.2 2.6 copy.45
  208.8 3.2 select_reduce_fusion
  212.6 2.3 select_add_fusion
  215.0 2.5 copy.46
  220.3 11.7 %cholesky.103 = f32[128,128]{1,0:T(8,128)S(1)} custom-call(f32[128,128]{1,0:T(8,128)S(1)} %cholesky.263), custom_call_target="Cholesky" | custom-call | tf_op jit(solution)/shard_map/jit(cholesky)/cholesky | solution.py:44
  232.0 9.8 %custom-call.34 = f32[1,128,128]{1,2,0:T(8,128)S(1)} custom-call(f32[1,128,128]{2,1,0:T(8,128)S(1)} %get-tuple-element.46), custom_call_target="InvertDiagBlocksLowerTriangular" | custom-call | tf_op jit(solution)/shard_map/jit(cholesky)/cholesky | solution.py:44
  244.4 11.7 %cholesky.215 = f32[128,128]{1,0:T(8,128)S(1)} custom-call(f32[128,128]{1,0:T(8,128)S(1)} %cholesky.267), custom_call_target="Cholesky" | custom-call | tf_op jit(solution)/shard_map/jit(cholesky)/cholesky | solution.py:44
  256.5 10.0 %custom-call.35 = f32[1,128,128]{1,2,0:T(8,128)S(1)} custom-call(f32[1,128,128]{2,1,0:T(8,128)S(1)} %get-tuple-element.44), custom_call_target="InvertDiagBlocksLowerTriangular" | custom-call | tf_op jit(solution)/shard_map/jit(cholesky)/cholesky | solution.py:44
  269.4 11.7 %cholesky.236 = f32[128,128]{1,0:T(8,128)S(1)} custom-call(f32[128,128]{1,0:T(8,128)S(1)} %cholesky.272), custom_call_target="Cholesky" | custom-call | tf_op jit(solution)/shard_map/jit(cholesky)/cholesky | solution.py:44
  281.9 9.8 %custom-call.36 = f32[1,128,128]{1,2,0:T(8,128)S(1)} custom-call(f32[1,128,128]{2,1,0:T(8,128)S(1)} %get-tuple-element.42), custom_call_target="InvertDiagBlocksLowerTriangular" | custom-call | tf_op jit(solution)/shard_map/jit(cholesky)/cholesky | solution.py:44
  294.2 11.9 %cholesky.253 = f32[128,128]{1,0:T(8,128)S(1)} custom-call(f32[128,128]{1,0:T(8,128)S(1)} %convolution_subtract_fusion.8), custom_call_target="Cholesky" | custom-call | tf_op jit(solution)/shard_map/jit(cholesky)/cholesky | solution.py:44
  312.1 2.4 select_select_fusion
  314.5 14.2 %while.1 = (s32[]{:T(128)}, f32[512,512]{0,1:T(8,128)}, s32[4,2]{0,1:T(2,128)S(1)}, f32[4,128,128]{2,1,0:T(8,128)}, s32[]{:T(128)}) while((s32[]{:T(128)}, f32[512,512]{0,1:T(8,128)}, s32[4,2]{0,1:T(2,128)S(1)}, f32[4,128,128]{2,1,0:T(8,128)}, s32[]{:T(128)}) %tuple.32), condition=%wide.while_cond, body=%wide.while_body.sunk | while | flops 2 | bytes 393829 | solution.py:45
  315.1 2.2 dynamic-slice.7
  322.2 2.2 dynamic-slice.7
  328.7 40.1 %custom-call.37 = f32[4,128,128]{1,2,0:T(8,128)S(1)} custom-call(f32[4,128,128]{2,1,0:T(8,128)} %get-tuple-element.12), custom_call_target="InvertDiagBlocksLowerTriangular" | custom-call | tf_op jit(solution)/shard_map/jit(_cho_solve)/triangular_solve | solution.py:45
  374.8 2.4 convolution_subtract_fusion.5
  380.6 3.1 fusion
  (109 shorter events, 43.3 us)
Async XLA Ops:
  6.5 3.2 copy-start
  6.5 159.3 %reduce-scatter.4.cloned.1.call-start = ((), (), s32[]{:S(2)}) async-start(), calls=%async_computation.3 | async-start | bytes 4325376 | tf_op jit(solution)/shard_map/reduce_scatter | solution.py:29
  14.2 3.8 copy-start.2
  18.0 147.9 %copy-start.7 = (s32[4]{0:T(128)S(1)}, s32[4]{0:T(128)}, u32[]{:S(2)}) copy-start(s32[4]{0:T(128)} %param.9) | copy-start | bytes 52
  18.0 150.6 %copy-start.1 = (s32[4]{0:T(128)S(1)}, s32[4]{0:T(128)}, u32[]{:S(2)}) copy-start(s32[4]{0:T(128)} %param.7) | copy-start | bytes 52
  18.0 151.3 %copy-start.9 = (f32[4]{0:T(128)S(1)}, f32[4]{0:T(128)}, u32[]{:S(2)}) copy-start(f32[4]{0:T(128)} %param.11) | copy-start | bytes 52
  18.0 152.6 %copy-start.8 = (s32[4,4]{1,0:T(4,128)S(1)}, s32[4,4]{1,0:T(4,128)}, u32[]{:S(2)}) copy-start(s32[4,4]{1,0:T(4,128)} %param.8) | copy-start | bytes 196
  18.1 155.0 %all-to-all-start = ((bf16[4,512,640]{2,1,0:T(8,128)(2,1)}), bf16[4,512,640]{2,1,0:T(8,128)(2,1)}, u32[]{:S(2)}, u32[]{:S(2)}) async-start(bf16[4,512,640]{2,1,0:T(8,128)(2,1)} %copy-done.2), calls=%async_computation | async-start | bytes 5242880 | tf_op jit(solution)/shard_map/all_to_all | solution.py:24
  22.8 183.4 %all-gather.2.cloned.1.call-start = ((), (), s32[]{:S(2)}) async-start(), calls=%async_computation.2 | async-start | bytes 1179648 | tf_op jit(solution)/shard_map/all_gather | solution.py:35
  219.3 1.0 copy-start.5
  266.9 1.0 copy-start.3
  368.8 5.9 %copy-start.4 = (f32[512,512]{0,1:T(8,128)S(1)}, f32[512,512]{0,1:T(8,128)}, u32[]{:S(2)}) copy-start(f32[512,512]{0,1:T(8,128)} %get-tuple-element.107) | copy-start | bytes 3145732
  378.0 2.6 copy-start.6
Sparse Core Ops, SparseCore 0:
  18.1 147.6 reduce-scatter.3
  168.0 38.1 all-gather.1
where the time goes:
time: 394 us; the launch traced here: 391 us
  waiting for transfers between devices  171 us (43%)
  other arithmetic  133 us (34%)
  local copies, waits for them, and re-layouts  35.5 us (9%)
  matrix products  25.2 us (6%)
  between operations  20.8 us (5%)
  starting transfers between devices  4.74 us (1%)
    reduce_scatter x1, waiting for transfers between devices, local(): lax.psum_scatter(partials.reshape(orbitals * domain_size, domain_size), (...  143 us
    another operation x15, other arithmetic, local(): jnp.linalg.cholesky(amplitude + level_shift * jnp.eye(domain_size, dtype=...  79.4 us
    another operation x3, other arithmetic, local(): solved = jax.scipy.linalg.cho_solve((factor, True), amplitude)  42.5 us
    all_gather x1, waiting for transfers between devices, local(): gram_sum = lax.all_gather(gram_part, 'aux', axis=0, tiled=True)  28.2 us
    another operation x20, local copies, waits for them, and re-layouts  14.2 us
    another operation x14, matrix products, local(): solved = jax.scipy.linalg.cho_solve((factor, True), amplitude)  11.6 us
  transfers between devices with their start and end apart: 3, of which 2 were waited for; matrix products, arithmetic and copies ran while one was open for 2% of the time, Pallas kernels for 0%

commit v1 on v0

--- a/solution.py
+++ b/solution.py
@@ -5,6 +5,20 @@
 
 LEVEL_RATIO = 0.5
 EPSILON = 1e-05
+
+
+def gates_rest(xx, in_dim):
+    p_count = jax.lax.axis_size("aux")
+    block_out = sorted(((nth, (nth + 1) % p_count) for nth in range(p_count)))
+    r_now = xx
+    by_place = [r_now]
+    for d in [*range(1, p_count)]:
+        r_now = jax.lax.ppermute(r_now, perm=block_out, axis_name="aux")
+        by_place.insert(0, r_now)
+    side_arr = jnp.concatenate(by_place, axis=in_dim)
+    after = jax.lax.axis_index("aux")
+    lower = after + 1
+    return jnp.roll(side_arr, lower * xx.shape[in_dim], in_dim)
 
 
 def local(pair_ints, domain_len, domain_blocks, slot_orbital, virt_energy, occ_energy):
@@ -32,7 +46,7 @@
         scatter_dimension=0,
         tiled=True,
     )
-    gram_sum = lax.all_gather(gram_part, "aux", axis=0, tiled=True)
+    gram_sum = gates_rest(gram_part, 0)
     energy_table = virt_energy.reshape(-1, block_rows)
     blocks = lax.dynamic_index_in_dim(domain_blocks, orbital, 0, keepdims=False)
     energies = jnp.take(energy_table, blocks, axis=0).reshape(domain_size)

time: 394 us -> 432 us (1.096)
  waiting for transfers between devices: 171 us -> 205 us
    unnamed x2, waiting for transfers between devices: 0.03 us -> 143 us
    reduce_scatter x1 -> x0, waiting for transfers between devices: 143 us -> none  [local(): lax.psum_scatter(partials.reshape(orbitals * domain_size, domain_size), (...]
    ppermute x0 -> x7, waiting for transfers between devices: none -> 61.4 us  [gates_rest(): r_now = jax.lax.ppermute(r_now, perm=block_out, axis_name='aux')]
    all_gather x1 -> x0, waiting for transfers between devices: 28.2 us -> none  [local(): gram_sum = lax.all_gather(gram_part, 'aux', axis=0, tiled=True)]
    concatenate x0 -> x1, local copies, waits for them, and re-layouts: none -> 4.81 us  [gates_rest(): return jnp.roll(side_arr, lower * xx.shape[in_dim], in_dim)]
  transfers between devices with their start and end apart: 3 -> 9, of which waited for: 2 -> 8; matrix products, arithmetic and copies ran while one was open for 2% -> 2% of each run, Pallas kernels for 0% -> 0%
where the time goes in v1:
time: 432 us; the launch traced here: 427 us
  waiting for transfers between devices  205 us (47%)
  other arithmetic  133 us (31%)
  local copies, waits for them, and re-layouts  39.2 us (9%)
  matrix products  25 us (6%)
  between operations  20.2 us (5%)
  starting transfers between devices  4.76 us (1%)
    unnamed x2, waiting for transfers between devices  143 us
    another operation x15, other arithmetic, local(): jnp.linalg.cholesky(amplitude + level_shift * jnp.eye(domain_size, dtype=...  79.4 us
    ppermute x7, waiting for transfers between devices, gates_rest(): r_now = jax.lax.ppermute(r_now, perm=block_out, axis_name='aux')  61.4 us
    another operation x3, other arithmetic, local(): solved = jax.scipy.linalg.cho_solve((factor, True), amplitude)  42.5 us
    another operation x20, local copies, waits for them, and re-layouts  14.4 us
    another operation x14, matrix products, local(): solved = jax.scipy.linalg.cho_solve((factor, True), amplitude)  11.5 us
  transfers between devices with their start and end apart: 9, of which 8 were waited for; matrix products, arithmetic and copies ran while one was open for 2% of the time, Pallas kernels for 0%

profile of v1, /device:TPU:0, one launch (start us, length us, event | category | flops | bytes accessed | tf_op | source)
XLA Modules:
  0.0 427.2 jit_solution(6648733664944130824)
XLA Ops:
  14.2 3.8 fusion.65
  18.1 4.7 %all-to-all-start = ((bf16[4,512,640]{2,1,0:T(8,128)(2,1)}), bf16[4,512,640]{2,1,0:T(8,128)(2,1)}, u32[]{:S(2)}, u32[]{:S(2)}) async-start(bf16[4,512,640]{2,1,0:T(8,128)(2,1)} %copy-done.2), calls=%async_computation | async-start | bytes 5242880 | tf_op jit(solution)/shard_map/all_to_all | solution.py:38
  22.8 143.3 %reduce-scatter.4.cloned.1.call-done = f32[64,512]{1,0:T(8,128)} async-done(((f32[2048,512]{1,0:T(8,128)}), f32[64,512]{1,0:T(8,128)}) %reduce-scatter.4.cloned.1.call-update) | async-done | bytes 131088
  167.1 9.1 %collective-permute-done = f32[64,512]{0,1:T(8,128)S(1)} collective-permute-done((f32[64,512]{0,1:T(8,128)S(1)}, f32[64,512]{0,1:T(8,128)S(1)}, u32[]{:S(2)}, u32[]{:S(2)}) %collective-permute-start) | collective-permute-done | bytes 131104 | tf_op jit(solution)/shard_map/ppermute | solution.py:16
  176.2 10.1 %collective-permute-done.1 = f32[64,512]{0,1:T(8,128)S(1)} collective-permute-done((f32[64,512]{0,1:T(8,128)S(1)}, f32[64,512]{0,1:T(8,128)S(1)}, u32[]{:S(2)}, u32[]{:S(2)}) %collective-permute-start.1) | collective-permute-done | bytes 131104 | tf_op jit(solution)/shard_map/ppermute | solution.py:16
  186.3 10.5 %collective-permute-done.2 = f32[64,512]{0,1:T(8,128)S(1)} collective-permute-done((f32[64,512]{0,1:T(8,128)S(1)}, f32[64,512]{0,1:T(8,128)S(1)}, u32[]{:S(2)}, u32[]{:S(2)}) %collective-permute-start.2) | collective-permute-done | bytes 131104 | tf_op jit(solution)/shard_map/ppermute | solution.py:16
  197.5 11.8 %collective-permute-done.3 = f32[64,512]{0,1:T(8,128)} collective-permute-done((f32[64,512]{0,1:T(8,128)S(1)}, f32[64,512]{0,1:T(8,128)}, u32[]{:S(2)}, u32[]{:S(2)}) %collective-permute-start.3) | collective-permute-done | bytes 131104 | tf_op jit(solution)/shard_map/ppermute | solution.py:16
  211.6 8.8 %collective-permute-done.4 = f32[64,512]{0,1:T(8,128)} collective-permute-done((f32[64,512]{0,1:T(8,128)}, f32[64,512]{0,1:T(8,128)}, u32[]{:S(2)}, u32[]{:S(2)}) %collective-permute-start.4) | collective-permute-done | bytes 131104 | tf_op jit(solution)/shard_map/ppermute | solution.py:16
  222.0 8.7 %collective-permute-done.5 = f32[64,512]{0,1:T(8,128)} collective-permute-done((f32[64,512]{0,1:T(8,128)}, f32[64,512]{0,1:T(8,128)}, u32[]{:S(2)}, u32[]{:S(2)}) %collective-permute-start.5) | collective-permute-done | bytes 131104 | tf_op jit(solution)/shard_map/ppermute | solution.py:16
  233.4 4.4 %copy.56 = bf16[1,512,4,640]{1,3,2,0:T(8,128)(2,1)} copy(bf16[1,512,4,640]{3,1,2,0:T(8,128)(2,1)} %bitcast.23) | data formatting | bytes 5242880 | tf_op jit(solution)/shard_map/all_to_all | solution.py:38
  237.7 2.4 collective-permute-done.6
  240.1 4.8 %concatenate.29 = f32[1024,512]{0,1:T(8,128)} concatenate(f32[64,512]{0,1:T(8,128)} %collective-permute-done.6, f32[64,512]{0,1:T(8,128)} %collective-permute-done.5, f32[64,512]{0,1:T(8,128)} %collective-permute-done.4, f32[64,512]{0,1:T(8,128)} %collective-permute-done.3, f32[64,512]{0,1:T(8,128)} %copy-done.8, f32[64,512]{0,1:T(8,128)S(1)} %collective-permute-done.1, ...), dimensions={0} | concatenate | bytes 4194304 | tf_op jit(solution)/shard_map/jit(_roll_dynamic)/concatenate | solution.py:21
  244.9 3.4 select_reduce_fusion
  251.3 2.6 copy.44
  256.6 11.7 %cholesky.103 = f32[128,128]{1,0:T(8,128)S(1)} custom-call(f32[128,128]{1,0:T(8,128)S(1)} %cholesky.263), custom_call_target="Cholesky" | custom-call | tf_op jit(solution)/shard_map/jit(cholesky)/cholesky | solution.py:58
  268.4 9.8 %custom-call.34 = f32[1,128,128]{1,2,0:T(8,128)S(1)} custom-call(f32[1,128,128]{2,1,0:T(8,128)S(1)} %get-tuple-element.46), custom_call_target="InvertDiagBlocksLowerTriangular" | custom-call | tf_op jit(solution)/shard_map/jit(cholesky)/cholesky | solution.py:58
  280.7 11.7 %cholesky.215 = f32[128,128]{1,0:T(8,128)S(1)} custom-call(f32[128,128]{1,0:T(8,128)S(1)} %cholesky.267), custom_call_target="Cholesky" | custom-call | tf_op jit(solution)/shard_map/jit(cholesky)/cholesky | solution.py:58
  292.8 10.0 %custom-call.35 = f32[1,128,128]{1,2,0:T(8,128)S(1)} custom-call(f32[1,128,128]{2,1,0:T(8,128)S(1)} %get-tuple-element.44), custom_call_target="InvertDiagBlocksLowerTriangular" | custom-call | tf_op jit(solution)/shard_map/jit(cholesky)/cholesky | solution.py:58
  305.8 11.7 %cholesky.236 = f32[128,128]{1,0:T(8,128)S(1)} custom-call(f32[128,128]{1,0:T(8,128)S(1)} %cholesky.272), custom_call_target="Cholesky" | custom-call | tf_op jit(solution)/shard_map/jit(cholesky)/cholesky | solution.py:58
  318.3 9.8 %custom-call.36 = f32[1,128,128]{1,2,0:T(8,128)S(1)} custom-call(f32[1,128,128]{2,1,0:T(8,128)S(1)} %get-tuple-element.42), custom_call_target="InvertDiagBlocksLowerTriangular" | custom-call | tf_op jit(solution)/shard_map/jit(cholesky)/cholesky | solution.py:58
  330.5 11.9 %cholesky.253 = f32[128,128]{1,0:T(8,128)S(1)} custom-call(f32[128,128]{1,0:T(8,128)S(1)} %convolution_subtract_fusion.5), custom_call_target="Cholesky" | custom-call | tf_op jit(solution)/shard_map/jit(cholesky)/cholesky | solution.py:58
  350.8 14.5 %while.1 = (s32[]{:T(128)}, f32[512,512]{0,1:T(8,128)}, s32[4,2]{0,1:T(2,128)S(1)}, f32[4,128,128]{2,1,0:T(8,128)}, s32[]{:T(128)}) while((s32[]{:T(128)}, f32[512,512]{0,1:T(8,128)}, s32[4,2]{0,1:T(2,128)S(1)}, f32[4,128,128]{2,1,0:T(8,128)}, s32[]{:T(128)}) %tuple.32), condition=%wide.while_cond, body=%wide.while_body.sunk | while | flops 2 | bytes 393829 | solution.py:59
  365.2 40.1 %custom-call.37 = f32[4,128,128]{1,2,0:T(8,128)S(1)} custom-call(f32[4,128,128]{2,1,0:T(8,128)} %get-tuple-element.12), custom_call_target="InvertDiagBlocksLowerTriangular" | custom-call | tf_op jit(solution)/shard_map/jit(_cho_solve)/triangular_solve | solution.py:59
  417.0 3.1 fusion
  (125 shorter events, 58.8 us)
Async XLA Ops:
  6.5 3.2 copy-start
  6.5 159.5 %reduce-scatter.4.cloned.1.call-start = ((), (), s32[]{:S(2)}) async-start(), calls=%async_computation.2 | async-start | bytes 4325376
  14.2 3.8 copy-start.2
  18.0 191.3 %copy-start.9 = (s32[4]{0:T(128)S(1)}, s32[4]{0:T(128)}, u32[]{:S(2)}) copy-start(s32[4]{0:T(128)} %param.9) | copy-start | bytes 52
  18.0 193.6 %copy-start.10 = (s32[4,4]{1,0:T(4,128)S(1)}, s32[4,4]{1,0:T(4,128)}, u32[]{:S(2)}) copy-start(s32[4,4]{1,0:T(4,128)} %param.8) | copy-start | bytes 196
  18.0 212.8 %copy-start.1 = (s32[4]{0:T(128)S(1)}, s32[4]{0:T(128)}, u32[]{:S(2)}) copy-start(s32[4]{0:T(128)} %param.7) | copy-start | bytes 52
  18.1 213.4 %copy-start.11 = (f32[4]{0:T(128)S(1)}, f32[4]{0:T(128)}, u32[]{:S(2)}) copy-start(f32[4]{0:T(128)} %param.11) | copy-start | bytes 52
  18.1 215.3 %all-to-all-start = ((bf16[4,512,640]{2,1,0:T(8,128)(2,1)}), bf16[4,512,640]{2,1,0:T(8,128)(2,1)}, u32[]{:S(2)}, u32[]{:S(2)}) async-start(bf16[4,512,640]{2,1,0:T(8,128)(2,1)} %copy-done.2), calls=%async_computation | async-start | bytes 5242880 | tf_op jit(solution)/shard_map/all_to_all | solution.py:38
  167.1 9.1 %collective-permute-start = (f32[64,512]{0,1:T(8,128)S(1)}, f32[64,512]{0,1:T(8,128)S(1)}, u32[]{:S(2)}, u32[]{:S(2)}) collective-permute-start(f32[64,512]{0,1:T(8,128)S(1)} %copy.63), channel_id=1, source_target_pairs={{0,1},{1,2},{2,3},{3,4},{4,5},{5,6},{6,7},{7,0},{8,9},{9,10},{10,1... | collective-permute-start | bytes 393224 | tf_op jit(solution)/shard_map/ppermute | solution.py:16
  176.2 10.1 %collective-permute-start.1 = (f32[64,512]{0,1:T(8,128)S(1)}, f32[64,512]{0,1:T(8,128)S(1)}, u32[]{:S(2)}, u32[]{:S(2)}) collective-permute-start(f32[64,512]{0,1:T(8,128)S(1)} %collective-permute-done), channel_id=1, source_target_pairs={{0,1},{1,2},{2,3},{3,4},{4,5},{5,6},{6,7},{7,0},{8,9},{9,10},{10,1... | collective-permute-start | bytes 393224 | tf_op jit(solution)/shard_map/ppermute | solution.py:16
  186.3 10.6 %collective-permute-start.2 = (f32[64,512]{0,1:T(8,128)S(1)}, f32[64,512]{0,1:T(8,128)S(1)}, u32[]{:S(2)}, u32[]{:S(2)}) collective-permute-start(f32[64,512]{0,1:T(8,128)S(1)} %collective-permute-done.1), channel_id=1, source_target_pairs={{0,1},{1,2},{2,3},{3,4},{4,5},{5,6},{6,7},{7,0},{8,9},{9,10},{10,1... | collective-permute-start | bytes 393224 | tf_op jit(solution)/shard_map/ppermute | solution.py:16
  196.8 0.7 copy-start.8
  197.5 11.8 %collective-permute-start.3 = (f32[64,512]{0,1:T(8,128)S(1)}, f32[64,512]{0,1:T(8,128)}, u32[]{:S(2)}, u32[]{:S(2)}) collective-permute-start(f32[64,512]{0,1:T(8,128)S(1)} %collective-permute-done.2), channel_id=1, source_target_pairs={{0,1},{1,2},{2,3},{3,4},{4,5},{5,6},{6,7},{7,0},{8,9},{9,10},{10,1... | collective-permute-start | bytes 393224 | tf_op jit(solution)/shard_map/ppermute | solution.py:16
  209.3 11.1 %collective-permute-start.4 = (f32[64,512]{0,1:T(8,128)}, f32[64,512]{0,1:T(8,128)}, u32[]{:S(2)}, u32[]{:S(2)}) collective-permute-start(f32[64,512]{0,1:T(8,128)} %collective-permute-done.3), channel_id=1, source_target_pairs={{0,1},{1,2},{2,3},{3,4},{4,5},{5,6},{6,7},{7,0},{8,9},{9,10},{10,1... | collective-permute-start | bytes 393224 | tf_op jit(solution)/shard_map/ppermute | solution.py:16
  220.5 10.3 %collective-permute-start.5 = (f32[64,512]{0,1:T(8,128)}, f32[64,512]{0,1:T(8,128)}, u32[]{:S(2)}, u32[]{:S(2)}) collective-permute-start(f32[64,512]{0,1:T(8,128)} %collective-permute-done.4), channel_id=1, source_target_pairs={{0,1},{1,2},{2,3},{3,4},{4,5},{5,6},{6,7},{7,0},{8,9},{9,10},{10,1... | collective-permute-start | bytes 393224 | tf_op jit(solution)/shard_map/ppermute | solution.py:16
  230.7 9.4 %collective-permute-start.6 = (f32[64,512]{0,1:T(8,128)}, f32[64,512]{0,1:T(8,128)}, u32[]{:S(2)}, u32[]{:S(2)}) collective-permute-start(f32[64,512]{0,1:T(8,128)} %collective-permute-done.5), channel_id=1, source_target_pairs={{0,1},{1,2},{2,3},{3,4},{4,5},{5,6},{6,7},{7,0},{8,9},{9,10},{10,1... | collective-permute-start | bytes 393224 | tf_op jit(solution)/shard_map/ppermute | solution.py:16
  255.6 1.0 copy-start.6
  303.3 1.0 copy-start.4
  405.4 6.3 %copy-start.3 = (f32[512,512]{0,1:T(8,128)S(1)}, f32[512,512]{0,1:T(8,128)}, u32[]{:S(2)}) copy-start(f32[512,512]{0,1:T(8,128)} %get-tuple-element.38) | copy-start | bytes 3145732
  405.4 6.7 %copy-start.5 = (f32[512,512]{0,1:T(8,128)S(1)}, f32[512,512]{0,1:T(8,128)}, u32[]{:S(2)}) copy-start(f32[512,512]{0,1:T(8,128)} %get-tuple-element.106) | copy-start | bytes 3145732
  414.4 2.6 copy-start.7
Sparse Core Ops, SparseCore 0:
  18.1 147.8 reduce-scatter.3
